TPU v7x, 32 devices: a whole 2x2x4 slice. The times are simulated.
32 devices in a mesh: dp: 8 (over z, y), tensor: 4 (over x, core).
Axes of the slice: x: 2, y: 2, z: 4, core: 2. Of those that a mesh axis runs over, the one named last changes fastest.
Arguments:
- tokens: bfloat16 [16384, 1536], P(('dp', 'tensor')), may hold values from -6 to 6
- segments: int32 [16384], P('dp'), may hold values from 0 to 3, as said below
- positions: int32 [16384], P('dp'), may hold values from 0 to 2044, as said below
- norm_attn: float32 [1536], replicated, may hold values from 0.1 to 1.9
- w_query: bfloat16 [1536, 1536], P(None, 'tensor'), may hold values from -0.15625 to 0.15625
- key_weight: bfloat16 [1536, 768], P(None, 'tensor'), may hold values from -0.15625 to 0.15625
- value_weight: bfloat16 [1536, 768], P(None, 'tensor'), may hold values from -0.15625 to 0.15625
- w_out: bfloat16 [1536, 1536], P('tensor'), may hold values from -1.5 to 1.5
- norm_mlp: float32 [1536], replicated, may hold values from 0.1 to 1.9
- w_gate: bfloat16 [1536, 4096], P(None, 'tensor'), may hold values from -0.15625 to 0.15625
- w_up: bfloat16 [1536, 4096], P(None, 'tensor'), may hold values from -0.15625 to 0.15625
- w_down: bfloat16 [4096, 1536], P('tensor'), may hold values from -0.09375 to 0.09375
- cotangent: bfloat16 [16384, 1536], P(('dp', 'tensor')), may hold values from -6 to 6
Outputs:
- output: bfloat16 [16384, 1536], P(('dp', 'tensor'))
- grad_tokens: float32 [16384, 1536], P(('dp', 'tensor'))
- grad_norm_attn: float32 [1536], replicated
- grad_w_query: float32 [1536, 1536], P(None, 'tensor')
- grad_w_key: float32 [1536, 768], P(None, 'tensor')
- grad_w_value: float32 [1536, 768], P(None, 'tensor')
- grad_w_out: float32 [1536, 1536], P('tensor')
- grad_norm_mlp: float32 [1536], replicated
- grad_w_gate: float32 [1536, 4096], P(None, 'tensor')
- grad_w_up: float32 [1536, 4096], P(None, 'tensor')
- grad_w_down: float32 [4096, 1536], P('tensor')
Inputs may be any that keep to these rules, and one draw needn't show every extreme that they name: `segments`: within each sequence of 2048 tokens the document numbers never fall, start at 0 and end at 3, each document one token or more. `positions`: each token's position within its document, 0 at the document's first token; the first sequence holds a document of 2045 tokens.
All inputs are finite; a program needn't handle non-finite values.
Results may differ from a plain program's by a relative error of at most 0.018.
Values may be sent and summed in bfloat16 or wider, within the bound.
A program may use at most 256 MiB of HBM per device.

v0:
```python
import math
import jax
import jax.numpy as jnp
from jax import lax
from jax.sharding import PartitionSpec as P

HEAD_SIZE = 96
epsilon = 1e-05
rope_base = 100000.0
masked_value = -1e30


def angle_tables(positions, width):
    middle = width // 2
    freq_steps = jnp.arange(middle, dtype=jnp.float32)
    inverse = jnp.exp(freq_steps * (-2.0 * math.log(rope_base) / width))
    angles = positions.astype(jnp.float32)[:, None] * inverse[None, :]
    return (jnp.cos(angles)[:, None, :], jnp.sin(angles)[:, None, :])


def apply_rotary(values, cosine_lookup, sine_lookup):
    middle = values.shape[-1] // 2
    front, second = (values[..., :middle], values[..., middle:])
    return jnp.concatenate(
        [
            front * cosine_lookup - second * sine_lookup,
            second * cosine_lookup + front * sine_lookup,
        ],
        axis=-1,
    )


def rotate_back(grads_in, cosine_lookup, sine_lookup):
    middle = grads_in.shape[-1] // 2
    front, second = (grads_in[..., :middle], grads_in[..., middle:])
    return jnp.concatenate(
        [
            front * cosine_lookup + second * sine_lookup,
            second * cosine_lookup - front * sine_lookup,
        ],
        axis=-1,
    )


def rms_inverse(values):
    return lax.rsqrt(jnp.mean(values * values, axis=-1, keepdims=True) + epsilon)


def norm_back(grad_normed, gain, unit_rows, inverse):
    scaled = grad_normed * gain
    return inverse * (scaled - unit_rows * jnp.mean(scaled * unit_rows, axis=-1, keepdims=True))


def contract_rows(left, right):
    return lax.dot_general(
        left, right, (((0,), (0,)), ((), ())), preferred_element_type=jnp.float32
    )


def contract_cols(left, right):
    return lax.dot_general(
        left, right, (((1,), (1,)), ((), ())), preferred_element_type=jnp.float32
    )


def block_scores(query_block, heads_of_key, allowed, score_scale):
    scores = (
        jnp.einsum("qgrd,kgd->grqk", query_block, heads_of_key, preferred_element_type=jnp.float32)
        * score_scale
    )
    return jnp.where(allowed[None, None], scores, masked_value)


def body(
    tokens,
    segments,
    positions,
    norm_attn,
    w_query,
    key_weight,
    value_weight,
    w_out,
    norm_mlp,
    w_gate,
    w_up,
    w_down,
    cotangent,
):
    sequence_length = segments.shape[0]
    q_heads = w_query.shape[1] // HEAD_SIZE
    kv_heads = key_weight.shape[1] // HEAD_SIZE
    head_repetitions = q_heads // kv_heads
    score_scale = 1.0 / math.sqrt(HEAD_SIZE)
    rows_per_block = min(512, sequence_length)
    block_total = sequence_length // rows_per_block
    cosine_lookup, sine_lookup = angle_tables(positions, HEAD_SIZE)
    indices = jnp.arange(sequence_length, dtype=jnp.int32)
    seg_blocks = segments.reshape(block_total, rows_per_block)
    index_blocks = indices.reshape(block_total, rows_per_block)
    inputs = tokens.astype(jnp.float32)
    inverse_one = rms_inverse(inputs)
    unit_one = inputs * inverse_one
    first_normalized = (unit_one * norm_attn).astype(jnp.bfloat16)
    attn_in = lax.all_gather(first_normalized, "tensor", axis=0, tiled=True)
    query_proj = jnp.dot(attn_in, w_query, preferred_element_type=jnp.float32).reshape(
        sequence_length, q_heads, HEAD_SIZE
    )
    key_proj = jnp.dot(attn_in, key_weight, preferred_element_type=jnp.float32).reshape(
        sequence_length, kv_heads, HEAD_SIZE
    )
    query_rows = apply_rotary(query_proj, cosine_lookup, sine_lookup).astype(jnp.bfloat16)
    heads_of_key = apply_rotary(key_proj, cosine_lookup, sine_lookup).astype(jnp.bfloat16)
    heads_of_value = (
        jnp.dot(attn_in, value_weight, preferred_element_type=jnp.float32)
        .astype(jnp.bfloat16)
        .reshape(sequence_length, kv_heads, HEAD_SIZE)
    )
    blocks_of_query = query_rows.reshape(
        block_total, rows_per_block, kv_heads, head_repetitions, HEAD_SIZE
    )

    def attend(member):
        query_block, rows_seg, rows_idx = member
        allowed = (rows_seg[:, None] == segments[None, :]) & (indices[None, :] <= rows_idx[:, None])
        scores = block_scores(query_block, heads_of_key, allowed, score_scale)
        row_peak = jnp.max(scores, axis=-1, keepdims=True)
        weights = jnp.exp(scores - row_peak)
        totals = jnp.sum(weights, axis=-1, keepdims=True)
        weights_low = (weights / totals).astype(jnp.bfloat16)
        mixed_heads = jnp.einsum(
            "grqk,kgd->qgrd", weights_low, heads_of_value, preferred_element_type=jnp.float32
        )
        return (mixed_heads.astype(jnp.bfloat16), row_peak[..., 0] + jnp.log(totals[..., 0]))

    attended, log_totals = lax.map(attend, (blocks_of_query, seg_blocks, index_blocks))
    attended = attended.reshape(sequence_length, q_heads * HEAD_SIZE)
    row_slice = attended
    attn_out = lax.psum_scatter(
        jnp.dot(row_slice, w_out, preferred_element_type=jnp.float32),
        "tensor",
        scatter_dimension=0,
        tiled=True,
    )
    hidden_one = inputs + attn_out
    inverse_two = rms_inverse(hidden_one)
    unit_two = hidden_one * inverse_two
    normed_two = (unit_two * norm_mlp).astype(jnp.bfloat16)
    mlp_in = lax.all_gather(normed_two, "tensor", axis=0, tiled=True)
    gate_proj = jnp.dot(mlp_in, w_gate, preferred_element_type=jnp.float32)
    up_proj = jnp.dot(mlp_in, w_up, preferred_element_type=jnp.float32)
    sigmoid_gate = jax.nn.sigmoid(gate_proj)
    activated = gate_proj * sigmoid_gate
    hidden = (activated * up_proj).astype(jnp.bfloat16)
    row_slice = hidden
    mlp_out = lax.psum_scatter(
        jnp.dot(row_slice, w_down, preferred_element_type=jnp.float32).astype(jnp.bfloat16),
        "tensor",
        scatter_dimension=0,
        tiled=True,
    ).astype(jnp.float32)
    output = (hidden_one + mlp_out).astype(jnp.bfloat16)
    grad_out = lax.all_gather(cotangent, "tensor", axis=0, tiled=True)
    grad_w_down = contract_rows(hidden, grad_out)
    grad_hidden = contract_cols(grad_out, w_down)
    grad_gate = (
        grad_hidden * up_proj * sigmoid_gate * (1.0 + gate_proj * (1.0 - sigmoid_gate))
    ).astype(jnp.bfloat16)
    grad_upper = (grad_hidden * activated).astype(jnp.bfloat16)
    grad_w_gate = contract_rows(mlp_in, grad_gate)
    grad_w_up = contract_rows(mlp_in, grad_upper)
    grad_normed_two = lax.psum_scatter(
        contract_cols(grad_gate, w_gate) + contract_cols(grad_upper, w_up),
        "tensor",
        scatter_dimension=0,
        tiled=True,
    )
    grad_norm_mlp = jnp.sum(grad_normed_two * unit_two, axis=0)
    grad_hidden_one = cotangent.astype(jnp.float32) + norm_back(
        grad_normed_two, norm_mlp, unit_two, inverse_two
    )
    grad_attn_rows = lax.all_gather(
        grad_hidden_one.astype(jnp.bfloat16), "tensor", axis=0, tiled=True
    )
    grad_w_out = contract_rows(attended, grad_attn_rows)
    grad_attended = contract_cols(grad_attn_rows, w_out).astype(jnp.bfloat16)
    grad_blocks = grad_attended.reshape(
        block_total, rows_per_block, kv_heads, head_repetitions, HEAD_SIZE
    )

    def attend_back(running, member):
        query_block, grad_block, rows_seg, rows_idx, log_block = member
        allowed = (rows_seg[:, None] == segments[None, :]) & (indices[None, :] <= rows_idx[:, None])
        scores = block_scores(query_block, heads_of_key, allowed, score_scale)
        weights = jnp.exp(scores - log_block[..., None])
        grad_weights = jnp.einsum(
            "qgrd,kgd->grqk", grad_block, heads_of_value, preferred_element_type=jnp.float32
        )
        inner_sum = jnp.sum(weights * grad_weights, axis=-1, keepdims=True)
        grad_scores = (weights * (grad_weights - inner_sum)).astype(jnp.bfloat16)
        grad_query = (
            jnp.einsum(
                "grqk,kgd->qgrd", grad_scores, heads_of_key, preferred_element_type=jnp.float32
            )
            * score_scale
        )
        grad_keys = (
            running[0]
            + jnp.einsum(
                "grqk,qgrd->kgd", grad_scores, query_block, preferred_element_type=jnp.float32
            )
            * score_scale
        )
        grad_values = running[1] + jnp.einsum(
            "grqk,qgrd->kgd",
            weights.astype(jnp.bfloat16),
            grad_block,
            preferred_element_type=jnp.float32,
        )
        return ((grad_keys, grad_values), grad_query)

    zero_state = jnp.zeros((sequence_length, kv_heads, HEAD_SIZE), jnp.float32)
    (grad_keys, grad_values), grad_queries = lax.scan(
        attend_back,
        (zero_state, zero_state),
        (blocks_of_query, grad_blocks, seg_blocks, index_blocks, log_totals),
    )
    grad_queries = grad_queries.reshape(sequence_length, q_heads, HEAD_SIZE)
    grad_q_proj = (
        rotate_back(grad_queries, cosine_lookup, sine_lookup)
        .reshape(sequence_length, q_heads * HEAD_SIZE)
        .astype(jnp.bfloat16)
    )
    grad_k_proj = (
        rotate_back(grad_keys, cosine_lookup, sine_lookup)
        .reshape(sequence_length, kv_heads * HEAD_SIZE)
        .astype(jnp.bfloat16)
    )
    grad_v_proj = grad_values.reshape(sequence_length, kv_heads * HEAD_SIZE).astype(jnp.bfloat16)
    grad_w_query = contract_rows(attn_in, grad_q_proj)
    grad_w_key = contract_rows(attn_in, grad_k_proj)
    grad_w_value = contract_rows(attn_in, grad_v_proj)
    grad_normed_one = lax.psum_scatter(
        (
            contract_cols(grad_q_proj, w_query)
            + contract_cols(grad_k_proj, key_weight)
            + contract_cols(grad_v_proj, value_weight)
        ).astype(jnp.bfloat16),
        "tensor",
        scatter_dimension=0,
        tiled=True,
    ).astype(jnp.float32)
    grad_norm_attn = jnp.sum(grad_normed_one * unit_one, axis=0)
    grad_tokens = grad_hidden_one + norm_back(grad_normed_one, norm_attn, unit_one, inverse_one)
    grad_norm_attn, grad_norm_mlp = lax.psum((grad_norm_attn, grad_norm_mlp), ("dp", "tensor"))
    grad_w_query, grad_w_key, grad_w_value, grad_w_out, grad_w_gate, grad_w_up, grad_w_down = (
        lax.psum(grad_w_query.astype(jnp.bfloat16), "dp").astype(jnp.float32),
        lax.psum(grad_w_key.astype(jnp.bfloat16), "dp").astype(jnp.float32),
        lax.psum(grad_w_value.astype(jnp.bfloat16), "dp").astype(jnp.float32),
        lax.psum(grad_w_out.astype(jnp.bfloat16), "dp").astype(jnp.float32),
        lax.psum(grad_w_gate.astype(jnp.bfloat16), "dp").astype(jnp.float32),
        lax.psum(grad_w_up.astype(jnp.bfloat16), "dp").astype(jnp.float32),
        lax.psum(grad_w_down.astype(jnp.bfloat16), "dp").astype(jnp.float32),
    )
    return (
        output,
        grad_tokens,
        grad_norm_attn,
        grad_w_query,
        grad_w_key,
        grad_w_value,
        grad_w_out,
        grad_norm_mlp,
        grad_w_gate,
        grad_w_up,
        grad_w_down,
    )


def solution(mesh):
    in_specs = (
        P(("dp", "tensor"), None),
        P("dp"),
        P("dp"),
        P(),
        P(None, "tensor"),
        P(None, "tensor"),
        P(None, "tensor"),
        P("tensor", None),
        P(),
        P(None, "tensor"),
        P(None, "tensor"),
        P("tensor", None),
        P(("dp", "tensor"), None),
    )
    out_specs = (
        P(("dp", "tensor"), None),
        P(("dp", "tensor"), None),
        P(),
        P(None, "tensor"),
        P(None, "tensor"),
        P(None, "tensor"),
        P("tensor", None),
        P(),
        P(None, "tensor"),
        P(None, "tensor"),
        P("tensor", None),
    )
    return jax.shard_map(body, mesh=mesh, in_specs=in_specs, out_specs=out_specs, check_vma=False)
```

profile of v0, /device:TPU:0, one launch (start us, length us, event | category | flops | bytes accessed | tf_op | source)
XLA Modules:
  0.0 1461.6 jit_solution(5925052065785356915)
XLA Ops:
  15.7 46.3 %all-gather.5.cloned.1.call-done = bf16[2048,1536]{1,0:T(8,128)(2,1)} async-done(((bf16[512,1536]{1,0:T(8,128)(2,1)}), bf16[2048,1536]{1,0:T(8,128)(2,1)}) %all-gather.5.cloned.1.call-update) | async-done | bytes 6291472 | tf_op jit(solution)/shard_map/all_gather | solution.py:104
  84.0 5.9 convolution_convert_fusion.9
  89.8 66.6 %while.28 = (s32[]{:T(128)}, bf16[4,512,2,2,96]{1,4,3,2,0:T(8,128)(2,1)}, f32[4,2,2,512]{3,2,1,0:T(2,128)}, s32[4,512]{1,0:T(4,128)S(1)}, s32[2048]{0:T(1024)S(1...) while((s32[]{:T(128)}, ...), condition=%wide.region_4.5_spmd.clone, body=%wide.region_1.4_spmd.clone.sunk | while | flops 1664284672 | bytes 60117144 | solution.py:135
  160.8 6.4 fusion.72
  167.2 99.1 %reduce-scatter.5.cloned.1.call-done = f32[512,1536]{1,0:T(8,128)} async-done(((f32[2048,1536]{1,0:T(8,128)}), f32[512,1536]{1,0:T(8,128)}) %reduce-scatter.5.cloned.1.call-update) | async-done | bytes 3145744 | tf_op jit(solution)/shard_map/reduce_scatter | solution.py:138
  273.0 45.9 %all-gather.7.cloned.1.call-done = bf16[2048,1536]{1,0:T(8,128)(2,1)} async-done(((bf16[512,1536]{1,0:T(8,128)(2,1)}), bf16[2048,1536]{1,0:T(8,128)(2,1)}) %all-gather.7.cloned.1.call-update) | async-done | bytes 6291472 | tf_op jit(solution)/shard_map/all_gather | solution.py:148
  318.9 12.6 fusion.74
  331.5 8.8 fusion.73
  340.3 26.4 %all-gather.9.cloned.1.call-done = bf16[2048,1536]{1,0:T(8,128)(2,1)} async-done(((bf16[512,1536]{1,0:T(8,128)(2,1)}), bf16[2048,1536]{1,0:T(8,128)(2,1)}) %all-gather.9.cloned.1.call-update) | async-done | bytes 6291472 | tf_op jit(solution)/shard_map/all_gather | solution.py:162
  366.8 18.8 %multiply_convert_fusion = (bf16[2048,1024]{1,0:T(8,128)(2,1)}, bf16[2048,1024]{1,0:T(8,128)(2,1)}, bf16[2048,1024]{1,0:T(8,128)(2,1)}) fusion(f32[2048,1024]{1,0:T(8,128)} %fusion.73, f32[2048,1024]{1,0:T(8,128)} %fusion.74, bf16[2048,1536]{1,0:T(8,128)(2,1)} %all-gather.9.cloned.1.call-done, bf16[1024,1536]{1,0:T(8,128)(2,1)S(1)} %copy-done), kind=kOutput, calls=%fused_computation.69 | convolution fusion | flops 6473908224 | bytes 38797312 | tf_op jit(solution)/shard_map/dot_general | solution.py:61
  385.6 11.6 fusion.75
  397.2 12.9 convolution_add_fusion
  410.1 99.1 %reduce-scatter.9.cloned.1.call-done = f32[512,1536]{1,0:T(8,128)} async-done(((f32[2048,1536]{1,0:T(8,128)}), f32[512,1536]{1,0:T(8,128)}) %reduce-scatter.9.cloned.1.call-update) | async-done | bytes 3145744 | tf_op jit(solution)/shard_map/reduce_scatter | solution.py:171
  517.6 46.5 %all-gather.11.cloned.1.call-done = bf16[2048,1536]{1,0:T(8,128)(2,1)} async-done(((bf16[512,1536]{1,0:T(8,128)(2,1)}), bf16[2048,1536]{1,0:T(8,128)(2,1)}) %all-gather.11.cloned.1.call-update) | async-done | bytes 6291472 | tf_op jit(solution)/shard_map/all_gather | solution.py:181
  564.1 7.7 convolution_convert_fusion.6
  571.8 7.0 reshape.300
  578.7 6.0 copy.29
  584.7 274.0 %while.29 = (s32[]{:T(128)}, f32[2048,2,96]{0,2,1:T(8,128)}, f32[2048,2,96]{0,2,1:T(8,128)}, f32[4,512,2,2,96]{1,0,4,3,2:T(4,128)}, bf16[4,512,2,2,96]{1,4,3,2,0...) while((s32[]{:T(128)}, f32[2048,2,96]{0,2,1:T(8,128)}, ...), condition=%wide.region_12.13_spmd.clone, body=%wide.region_10.12_spmd.clone.sunk | while | flops 4094752768 | bytes 214511840 | solution.py:222
  590.7 5.8 copy-done.1
  596.5 7.1 fusion.158
  603.6 12.6 fusion.155
  616.3 12.2 fusion.156
  636.6 16.1 %dynamic_update_slice.22 = f32[4,512,2,2,96]{1,0,4,3,2:T(4,128)} dynamic-update-slice(f32[4,512,2,2,96]{1,0,4,3,2:T(4,128)} %get-tuple-element.503, f32[1,512,2,2,96]{1,0,4,3,2:T(1,128)} %copy.49, s32[]{:T(128)S(6)} %copy.66, s32[]{:T(128)} %constant.58.clone.1..sunk, s32[]{:T(128)} %constant.58.clone.1..sunk, s32[]{:T(128)} %constant.58.clone.1..sunk, s32[]{:T(128)} %constant.58.clone.1..sunk) | dynamic-update-slice | bytes 1572868 | tf_op jit(solution)/shard_map/while/body/jit(dynamic_update_index_in_dim)/dynamic_update_slice | solution.py:222
  664.0 7.7 fusion.158
  671.7 12.6 fusion.155
  684.3 12.2 fusion.156
  705.2 16.1 %dynamic_update_slice.22 = f32[4,512,2,2,96]{1,0,4,3,2:T(4,128)} dynamic-update-slice(f32[4,512,2,2,96]{1,0,4,3,2:T(4,128)} %get-tuple-element.503, f32[1,512,2,2,96]{1,0,4,3,2:T(1,128)} %copy.49, s32[]{:T(128)S(6)} %copy.66, s32[]{:T(128)} %constant.58.clone.1..sunk, s32[]{:T(128)} %constant.58.clone.1..sunk, s32[]{:T(128)} %constant.58.clone.1..sunk, s32[]{:T(128)} %constant.58.clone.1..sunk) | dynamic-update-slice | bytes 1572868 | tf_op jit(solution)/shard_map/while/body/jit(dynamic_update_index_in_dim)/dynamic_update_slice | solution.py:222
  726.9 5.8 copy-done.1
  732.7 7.7 fusion.158
  740.3 12.6 fusion.155
  753.0 12.2 fusion.156
  773.8 16.1 %dynamic_update_slice.22 = f32[4,512,2,2,96]{1,0,4,3,2:T(4,128)} dynamic-update-slice(f32[4,512,2,2,96]{1,0,4,3,2:T(4,128)} %get-tuple-element.503, f32[1,512,2,2,96]{1,0,4,3,2:T(1,128)} %copy.49, s32[]{:T(128)S(6)} %copy.66, s32[]{:T(128)} %constant.58.clone.1..sunk, s32[]{:T(128)} %constant.58.clone.1..sunk, s32[]{:T(128)} %constant.58.clone.1..sunk, s32[]{:T(128)} %constant.58.clone.1..sunk) | dynamic-update-slice | bytes 1572868 | tf_op jit(solution)/shard_map/while/body/jit(dynamic_update_index_in_dim)/dynamic_update_slice | solution.py:222
  795.5 5.8 copy-done.1
  801.3 7.7 fusion.158
  809.0 12.6 fusion.155
  821.6 12.2 fusion.156
  842.5 16.1 %dynamic_update_slice.22 = f32[4,512,2,2,96]{1,0,4,3,2:T(4,128)} dynamic-update-slice(f32[4,512,2,2,96]{1,0,4,3,2:T(4,128)} %get-tuple-element.503, f32[1,512,2,2,96]{1,0,4,3,2:T(1,128)} %copy.49, s32[]{:T(128)S(6)} %copy.66, s32[]{:T(128)} %constant.58.clone.1..sunk, s32[]{:T(128)} %constant.58.clone.1..sunk, s32[]{:T(128)} %constant.58.clone.1..sunk, s32[]{:T(128)} %constant.58.clone.1..sunk) | dynamic-update-slice | bytes 1572868 | tf_op jit(solution)/shard_map/while/body/jit(dynamic_update_index_in_dim)/dynamic_update_slice | solution.py:222
  870.0 6.5 fusion.76
  876.6 6.4 fusion.77
  883.0 12.8 add_convert_fusion
  895.9 10.9 convolution_convert_fusion
  906.9 12.0 convolution_convert_fusion.2
  919.0 10.1 convolution_convert_fusion.3
  929.1 8.5 convolution_convert_fusion.1
  957.3 40.1 %all-reduce = (f32[1536]{0:T(1024)}, f32[1536]{0:T(1024)}) all-reduce(f32[1536]{0:T(1024)S(1)} %get-tuple-element.234, f32[1536]{0:T(1024)S(1)} %copy-done.41), channel_id=1, replica_groups=mesh['dp'=8,'tensor'=4] {'dp','tensor'}, use_global_device_ids=true, to_apply=%region_16.17 | all-reduce | flops 3072 | bytes 24576 | tf_op jit(solution)/shard_map/psum | solution.py:254
  997.4 19.3 %reduce-scatter.7.cloned.1.call-done = bf16[512,1536]{1,0:T(8,128)(2,1)} async-done(((bf16[2048,1536]{1,0:T(8,128)(2,1)}), bf16[512,1536]{1,0:T(8,128)(2,1)}) %reduce-scatter.7.cloned.1.call-update) | async-done | bytes 1572880 | tf_op jit(solution)/shard_map/reduce_scatter | solution.py:155
  1016.7 7.0 fusion.64
  1023.7 413.4 %all-reduce.4.cloned.1.call-done = (bf16[1536,384]{1,0:T(8,128)(2,1)}, bf16[1536,192]{0,1:T(8,128)(2,1)}, bf16[1536,192]{0,1:T(8,128)(2,1)}, bf16[384,1536]{1,0:...) async-done(((bf16[1536,384]{1,0:T(8,128)(2,1)}, bf16[1536,192]{0,1:T(8,128)(2,1)}, bf16[1536,192]{0,1:T(8,128)(2,1)}, ...) | async-done | bytes 12976144 | tf_op jit(solution)/shard_map/psum | solution.py:256
  (260 shorter events, 226.5 us)
Async XLA Ops:
  7.2 359.6 %copy-start = (bf16[1024,1536]{1,0:T(8,128)(2,1)S(1)}, bf16[1024,1536]{1,0:T(8,128)(2,1)}, u32[]{:S(2)}) copy-start(bf16[1024,1536]{1,0:T(8,128)(2,1)} %param.28) | copy-start | bytes 9437188
  7.2 5.7 copy-start.29
  7.2 5.7 copy-start.46
  7.2 54.8 %all-gather.5.cloned.1.call-start = ((), (), s32[]{:S(2)}) async-start(), calls=%async_computation.4 | async-start | bytes 7864320 | tf_op jit(solution)/shard_map/all_gather | solution.py:104
  12.8 253.6 %reduce-scatter.5.cloned.1.call-start = ((), (), s32[]{:S(2)}) async-start(), calls=%async_computation.5 | async-start | bytes 15728640 | tf_op jit(solution)/shard_map/reduce_scatter | solution.py:138
  15.7 55.7 %copy-start.7 = (f32[2048,48]{0,1:T(8,128)}, f32[2048,48]{0,1:T(8,128)S(1)}, u32[]{:S(2)}) copy-start(f32[2048,48]{0,1:T(8,128)S(1)} %get-tuple-element.310) | copy-start | bytes 1179652
  62.0 6.4 copy-start.47
  84.0 5.9 copy-start.37
  167.2 103.7 %copy-start.35 = (f32[1536]{0:T(1024)S(1)}, f32[1536]{0:T(1024)}, u32[]{:S(2)}) copy-start(f32[1536]{0:T(1024)} %param.25) | copy-start | bytes 18436
  167.2 151.7 %all-gather.7.cloned.1.call-start = ((), (), s32[]{:S(2)}) async-start(), calls=%async_computation.6 | async-start | bytes 7864320 | tf_op jit(solution)/shard_map/all_gather | solution.py:148
  269.2 244.4 %copy-start.39 = (f32[512]{0:T(512)}, f32[512]{0:T(512)S(1)}, u32[]{:S(2)}) copy-start(f32[512]{0:T(512)S(1)} %add_rsqrt_fusion) | copy-start | bytes 6148
  272.4 94.4 %all-gather.9.cloned.1.call-start = ((), (), s32[]{:S(2)}) async-start(), calls=%async_computation.8 | async-start | bytes 7864320 | tf_op jit(solution)/shard_map/all_gather | solution.py:162
  273.0 236.3 %reduce-scatter.9.cloned.1.call-start = ((), (), s32[]{:S(2)}) async-start(), calls=%async_computation.9 | async-start | bytes 15728640 | tf_op jit(solution)/shard_map/reduce_scatter | solution.py:171
  318.9 12.6 copy-start.48
  318.9 12.6 copy-start.49
  366.8 18.8 %copy-start.50 = (bf16[1536,1024]{1,0:T(8,128)(2,1)S(1)}, bf16[1536,1024]{1,0:T(8,128)(2,1)}, u32[]{:S(2)}) copy-start(bf16[1536,1024]{1,0:T(8,128)(2,1)} %param.26) | copy-start | bytes 9437188
  385.5 11.6 copy-start.51
  385.5 11.6 copy-start.53
  410.1 154.0 %all-gather.11.cloned.1.call-start = ((), (), s32[]{:S(2)}) async-start(), calls=%async_computation.10 | async-start | bytes 7864320 | tf_op jit(solution)/shard_map/all_gather | solution.py:181
  517.5 436.8 %reduce-scatter.11.cloned.1.call-start = ((), (), s32[]{:S(2)}) async-start(), calls=%async_computation.11 | async-start | bytes 7864320 | tf_op jit(solution)/shard_map/reduce_scatter | solution.py:242
  590.7 5.8 copy-start.1
  616.2 12.2 copy-start.2
  658.2 5.8 copy-start.1
  684.3 12.2 copy-start.2
  726.9 5.8 copy-start.1
  753.0 12.2 copy-start.2
  795.5 5.8 copy-start.1
  821.6 12.2 copy-start.2
  858.7 5.3 copy-start.8
  868.4 14.7 %copy-start.20 = (bf16[2048,2,96]{0,2,1:T(8,128)(2,1)}, bf16[2048,2,96]{0,2,1:T(8,128)(2,1)S(1)}, u32[]{:S(2)}) copy-start(bf16[2048,2,96]{0,2,1:T(8,128)(2,1)S(1)} %convert_element_type.138) | copy-start | bytes 2359300
  868.5 8.0 copy-start.13
  870.0 6.6 copy-start.32
  876.6 6.4 copy-start.15
  876.6 6.4 copy-start.34
  895.8 120.9 %reduce-scatter.7.cloned.1.call-start = ((), (), s32[]{:S(2)}) async-start(), calls=%async_computation.7 | async-start | bytes 7864320 | tf_op jit(solution)/shard_map/reduce_scatter | solution.py:155
  906.8 530.3 %all-reduce.4.cloned.1.call-start = ((), (), s32[]{:S(2)}) async-start(), calls=%async_computation.12 | async-start | bytes 25952256 | tf_op jit(solution)/shard_map/psum | solution.py:256
  906.9 12.1 copy-start.52
  906.9 22.2 %slice-start.2 = ((s8[6291456]{0:T(1024)(128)(4,1)}), s8[4194304]{0:T(1024)(128)(4,1)S(1)}, s32[]{:S(2)}) async-start(s8[6291456]{0:T(1024)(128)(4,1)} %bitcast.262), calls=%async_computation.15 | async-start | bytes 8388608
  918.9 10.2 slice-start.3
  918.9 10.2 copy-start.54
  918.9 18.7 %slice-start = ((s8[6291456]{0:T(1024)(128)(4,1)}), s8[4194304]{0:T(1024)(128)(4,1)S(1)}, s32[]{:S(2)}) async-start(s8[6291456]{0:T(1024)(128)(4,1)} %bitcast.260), calls=%async_computation.13 | async-start | bytes 8388608
  929.1 8.6 copy-start.16
  929.1 8.6 slice-start.1
  950.4 6.9 copy-start.41
  950.4 66.3 %copy-start.36 = (f32[1536]{0:T(1024)S(1)}, f32[1536]{0:T(1024)}, u32[]{:S(2)}) copy-start(f32[1536]{0:T(1024)} %param.25) | copy-start | bytes 18436
  950.4 66.3 %copy-start.40 = (f32[512]{0:T(512)S(1)}, f32[512]{0:T(512)}, u32[]{:S(2)}) copy-start(f32[512]{0:T(512)} %copy-done.39) | copy-start | bytes 6148
  950.4 66.3 %copy-start.45 = (f32[512]{0:T(512)S(1)}, f32[512]{0:T(512)}, u32[]{:S(2)}) copy-start(f32[512]{0:T(512)} %copy-done.44) | copy-start | bytes 6148
  1437.1 5.3 copy-start.25
  (31 other events, 104.4 us)
Sparse Core Ops, SparseCore 0:
  12.9 49.0 all-gather.4
  167.3 99.0 reduce-scatter.4
  272.5 46.3 all-gather.6
  320.3 46.3 all-gather.8
  410.2 99.0 reduce-scatter.8
  517.7 46.3 all-gather.10
  895.9 58.3 reduce-scatter.10
  957.6 59.0 reduce-scatter.6
  1023.5 413.5 all-reduce.3
where the time goes:
time: 1470 us; the launch traced here: 1460 us
  waiting for transfers between devices  801 us (54%)
  matrix products  336 us (23%)
  other arithmetic  136 us (9%)
  local copies, waits for them, and re-layouts  132 us (9%)
  blocking collectives  40.1 us (3%)
  between operations  14.9 us (1%)
    psum x1, waiting for transfers between devices, body(): lax.psum(grad_w_query.astype(jnp.bfloat16), 'dp').astype(jnp.float32)  413 us
    reduce_scatter x1, waiting for transfers between devices, body(): lax.psum_scatter(contract_cols(grad_gate, w_gate) + contract_cols(grad_up...  99.1 us
    reduce_scatter x1, waiting for transfers between devices, body(): lax.psum_scatter(jnp.dot(row_slice, w_out, preferred_element_type=jnp.flo...  99.1 us
    dot_general x7, matrix products, contract_cols(): lax.dot_general(left, right, (((1,), (1,)), ((), ())), preferred_element_...  76.6 us
    dynamic_update_slice x8, local copies, waits for them, and re-layouts, body(): lax.scan(attend_back, (zero_state, zero_state), (blocks_of_query, grad_bl...  71.2 us
    dot_general x4, matrix products, attend_back(): jnp.einsum('qgrd,kgd->grqk', grad_block, heads_of_value, preferred_elemen...  50.6 us
    convert_element_type x4, other arithmetic, attend_back(): grad_scores = (weights * (grad_weights - inner_sum)).astype(jnp.bfloat16)  48.7 us
    all_gather x1, waiting for transfers between devices, body(): lax.all_gather(grad_hidden_one.astype(jnp.bfloat16), 'tensor', axis=0, ti...  46.5 us
  transfers between devices with their start and end apart: 9, of which 9 were waited for; matrix products, arithmetic and copies ran while one was open for 6% of the time, Pallas kernels for 0%

commit v1 on v0

--- a/solution.py
+++ b/solution.py
@@ -145,7 +145,23 @@
     inverse_two = rms_inverse(hidden_one)
     unit_two = hidden_one * inverse_two
     normed_two = (unit_two * norm_mlp).astype(jnp.bfloat16)
-    mlp_in = lax.all_gather(normed_two, "tensor", axis=0, tiled=True)
+    ways, here, step = (lax.axis_size("tensor"), lax.axis_index("tensor"), normed_two.shape[0])
+    shape = [n * ways if d == 0 else n for d, n in enumerate(normed_two.shape)]
+    full = lax.dynamic_update_slice_in_dim(
+        jnp.zeros(shape, normed_two.dtype), normed_two, here * step, axis=0
+    )
+    going_up = going_down = normed_two
+    for far in range(1, ways // 2 + 1):
+        going_up = lax.ppermute(going_up, "tensor", [(d, (d + 1) % ways) for d in range(ways)])
+        full = lax.dynamic_update_slice_in_dim(full, going_up, (here - far) % ways * step, axis=0)
+        if 2 * far < ways:
+            going_down = lax.ppermute(
+                going_down, "tensor", [(d, (d - 1) % ways) for d in range(ways)]
+            )
+            full = lax.dynamic_update_slice_in_dim(
+                full, going_down, (here + far) % ways * step, axis=0
+            )
+    mlp_in = full
     gate_proj = jnp.dot(mlp_in, w_gate, preferred_element_type=jnp.float32)
     up_proj = jnp.dot(mlp_in, w_up, preferred_element_type=jnp.float32)
     sigmoid_gate = jax.nn.sigmoid(gate_proj)

time: 1470 us -> 1450 us (0.986)
  local copies, waits for them, and re-layouts: 132 us -> 115 us
    ppermute x0 -> x3, waiting for transfers between devices: none -> 67.5 us  [the longest x2 67.5 us: body(): lax.ppermute(going_up, 'tensor', [(d, (d + 1) % ways) for d in range(ways)])]
    all_gather x1 -> x0, waiting for transfers between devices: 45.9 us -> none  [body(): mlp_in = lax.all_gather(normed_two, 'tensor', axis=0, tiled=True)]
    while x24 -> x64, local copies, waits for them, and re-layouts: 23.2 us -> 0.16 us
    all_gather x1, waiting for transfers between devices: 26.4 us -> 3.56 us  [body(): grad_out = lax.all_gather(cotangent, 'tensor', axis=0, tiled=True)]
  transfers between devices with their start and end apart: 9 -> 11, of which waited for: 9 -> 9; matrix products, arithmetic and copies ran while one was open for 6% -> 6% of each run, Pallas kernels for 0% -> 0%
where the time goes in v1:
time: 1450 us; the launch traced here: 1440 us
  waiting for transfers between devices  799 us (55%)
  matrix products  338 us (23%)
  other arithmetic  130 us (9%)
  local copies, waits for them, and re-layouts  115 us (8%)
  blocking collectives  40 us (3%)
  between operations  15 us (1%)
    psum x1, waiting for transfers between devices, body(): lax.psum(grad_w_query.astype(jnp.bfloat16), 'dp').astype(jnp.float32)  414 us
    reduce_scatter x1, waiting for transfers between devices, body(): lax.psum_scatter(contract_cols(grad_gate, w_gate) + contract_cols(grad_up...  98.7 us
    reduce_scatter x1, waiting for transfers between devices, body(): lax.psum_scatter(jnp.dot(row_slice, w_out, preferred_element_type=jnp.flo...  98.4 us
    ppermute x2, waiting for transfers between devices, body(): lax.ppermute(going_up, 'tensor', [(d, (d + 1) % ways) for d in range(ways)])  67.5 us
    dynamic_update_slice x8, local copies, waits for them, and re-layouts, body(): lax.scan(attend_back, (zero_state, zero_state), (blocks_of_query, grad_bl...  67.5 us
    dot_general x7, matrix products, contract_cols(): lax.dot_general(left, right, (((1,), (1,)), ((), ())), preferred_element_...  66.9 us
    all_gather x1, waiting for transfers between devices, body(): lax.all_gather(grad_hidden_one.astype(jnp.bfloat16), 'tensor', axis=0, ti...  46.5 us
    all_gather x1, waiting for transfers between devices, body(): attn_in = lax.all_gather(first_normalized, 'tensor', axis=0, tiled=True)  46.3 us
  transfers between devices with their start and end apart: 11, of which 9 were waited for; matrix products, arithmetic and copies ran while one was open for 6% of the time, Pallas kernels for 0%

profile of v1, /device:TPU:0, one launch (start us, length us, event | category | flops | bytes accessed | tf_op | source)
XLA Modules:
  0.0 1440.3 jit_solution(12531182972081298498)
XLA Ops:
  15.2 46.3 %all-gather.4.cloned.1.call-done = bf16[2048,1536]{1,0:T(8,128)(2,1)} async-done(((bf16[512,1536]{1,0:T(8,128)(2,1)}), bf16[2048,1536]{1,0:T(8,128)(2,1)}) %all-gather.4.cloned.1.call-update) | async-done | bytes 6291472 | tf_op jit(solution)/shard_map/all_gather | solution.py:104
  83.4 5.8 convolution_convert_fusion.9
  89.2 69.3 %while.28 = (s32[]{:T(128)}, bf16[4,512,2,2,96]{1,4,3,2,0:T(8,128)(2,1)}, f32[4,2,2,512]{3,2,1,0:T(2,128)}, s32[4,512]{1,0:T(4,128)S(1)}, s32[2048]{0:T(1024)S(1...) while((s32[]{:T(128)}, ...), condition=%wide.region_4.5_spmd.clone, body=%wide.region_1.4_spmd.clone.sunk | while | flops 1664284672 | bytes 60117144 | solution.py:135
  135.0 5.6 fusion.144
  162.9 6.4 fusion.72
  170.1 98.4 %reduce-scatter.5.cloned.1.call-done = f32[512,1536]{1,0:T(8,128)} async-done(((f32[2048,1536]{1,0:T(8,128)}), f32[512,1536]{1,0:T(8,128)}) %reduce-scatter.5.cloned.1.call-update) | async-done | bytes 3145744 | tf_op jit(solution)/shard_map/reduce_scatter | solution.py:138
  279.0 67.5 %collective-permute-done = bf16[512,1536]{1,0:T(8,128)(2,1)} collective-permute-done((bf16[512,1536]{1,0:T(8,128)(2,1)}, bf16[512,1536]{1,0:T(8,128)(2,1)}, u32[]{:S(2)}, u32[]{:S(2)}) %collective-permute-start) | collective-permute-done | bytes 1572896 | tf_op jit(solution)/shard_map/ppermute | solution.py:155
  350.1 12.6 fusion.74
  370.8 11.3 fusion.73
  382.1 16.4 %multiply_convert_fusion = (bf16[2048,1024]{1,0:T(8,128)(2,1)}, bf16[2048,1024]{1,0:T(8,128)(2,1)}, bf16[2048,1024]{1,0:T(8,128)(2,1)}) fusion(f32[2048,1024]{1,0:T(8,128)} %fusion.74, f32[2048,1024]{1,0:T(8,128)} %fusion.73, bf16[2048,1536]{1,0:T(8,128)(2,1)S(1)} %copy-done.17, bf16[1536,1024]{1,0:T(8,128)(2,1)S(1)} %copy-done), kind=kOutput, calls=%fused_computation.69 | convolution fusion | flops 6473908224 | bytes 38797312 | tf_op jit(solution)/shard_map/dot_general | solution.py:165
  398.5 8.7 fusion.75
  407.2 12.3 convolution_add_fusion
  419.6 98.7 %reduce-scatter.9.cloned.1.call-done = f32[512,1536]{1,0:T(8,128)} async-done(((f32[2048,1536]{1,0:T(8,128)}), f32[512,1536]{1,0:T(8,128)}) %reduce-scatter.9.cloned.1.call-update) | async-done | bytes 3145744 | tf_op jit(solution)/shard_map/reduce_scatter | solution.py:187
  523.9 46.5 %all-gather.8.cloned.1.call-done = bf16[2048,1536]{1,0:T(8,128)(2,1)} async-done(((bf16[512,1536]{1,0:T(8,128)(2,1)}), bf16[2048,1536]{1,0:T(8,128)(2,1)}) %all-gather.8.cloned.1.call-update) | async-done | bytes 6291472 | tf_op jit(solution)/shard_map/all_gather | solution.py:197
  570.3 7.7 convolution_convert_fusion.6
  578.0 6.3 reshape.300
  588.7 252.2 %while.29 = (s32[]{:T(128)}, f32[2048,2,96]{0,2,1:T(8,128)}, f32[2048,2,96]{0,2,1:T(8,128)}, f32[4,512,2,2,96]{1,0,4,3,2:T(4,128)}, bf16[4,512,2,2,96]{1,4,3,2,0...) while((s32[]{:T(128)}, f32[2048,2,96]{0,2,1:T(8,128)}, ...), condition=%wide.region_12.13_spmd.clone, body=%wide.region_10.12_spmd.clone.sunk | while | flops 4094752768 | bytes 190525824 | solution.py:238
  595.9 7.2 fusion.158
  603.1 11.3 fusion.155
  614.4 10.9 fusion.156
  625.4 6.4 fusion.159
  635.4 16.1 %dynamic_update_slice.42 = f32[4,512,2,2,96]{1,0,4,3,2:T(4,128)} dynamic-update-slice(f32[4,512,2,2,96]{1,0,4,3,2:T(4,128)} %get-tuple-element.505, f32[1,512,2,2,96]{1,0,4,3,2:T(1,128)S(1)} %copy.49, s32[]{:T(128)S(6)} %copy.70, s32[]{:T(128)} %constant.86.clone.1..sunk, s32[]{:T(128)} %constant.86.clone.1..sunk, s32[]{:T(128)} %constant.86.clone.1..sunk, s32[]{:T(128)} %constant.86.clone.1..sunk) | dynamic-update-slice | bytes 1572868 | tf_op jit(solution)/shard_map/while/body/jit(dynamic_update_index_in_dim)/dynamic_update_slice | solution.py:238
  658.4 7.7 fusion.158
  666.2 11.3 fusion.155
  677.5 10.9 fusion.156
  688.5 6.4 fusion.159
  698.5 16.1 %dynamic_update_slice.42 = f32[4,512,2,2,96]{1,0,4,3,2:T(4,128)} dynamic-update-slice(f32[4,512,2,2,96]{1,0,4,3,2:T(4,128)} %get-tuple-element.505, f32[1,512,2,2,96]{1,0,4,3,2:T(1,128)S(1)} %copy.49, s32[]{:T(128)S(6)} %copy.70, s32[]{:T(128)} %constant.86.clone.1..sunk, s32[]{:T(128)} %constant.86.clone.1..sunk, s32[]{:T(128)} %constant.86.clone.1..sunk, s32[]{:T(128)} %constant.86.clone.1..sunk) | dynamic-update-slice | bytes 1572868 | tf_op jit(solution)/shard_map/while/body/jit(dynamic_update_index_in_dim)/dynamic_update_slice | solution.py:238
  721.5 7.7 fusion.158
  729.3 11.3 fusion.155
  740.6 10.9 fusion.156
  751.6 6.4 fusion.159
  761.6 16.1 %dynamic_update_slice.42 = f32[4,512,2,2,96]{1,0,4,3,2:T(4,128)} dynamic-update-slice(f32[4,512,2,2,96]{1,0,4,3,2:T(4,128)} %get-tuple-element.505, f32[1,512,2,2,96]{1,0,4,3,2:T(1,128)S(1)} %copy.49, s32[]{:T(128)S(6)} %copy.70, s32[]{:T(128)} %constant.86.clone.1..sunk, s32[]{:T(128)} %constant.86.clone.1..sunk, s32[]{:T(128)} %constant.86.clone.1..sunk, s32[]{:T(128)} %constant.86.clone.1..sunk) | dynamic-update-slice | bytes 1572868 | tf_op jit(solution)/shard_map/while/body/jit(dynamic_update_index_in_dim)/dynamic_update_slice | solution.py:238
  784.6 7.7 fusion.158
  792.4 11.3 fusion.155
  803.7 10.9 fusion.156
  814.7 6.4 fusion.159
  824.7 16.1 %dynamic_update_slice.42 = f32[4,512,2,2,96]{1,0,4,3,2:T(4,128)} dynamic-update-slice(f32[4,512,2,2,96]{1,0,4,3,2:T(4,128)} %get-tuple-element.505, f32[1,512,2,2,96]{1,0,4,3,2:T(1,128)S(1)} %copy.49, s32[]{:T(128)S(6)} %copy.70, s32[]{:T(128)} %constant.86.clone.1..sunk, s32[]{:T(128)} %constant.86.clone.1..sunk, s32[]{:T(128)} %constant.86.clone.1..sunk, s32[]{:T(128)} %constant.86.clone.1..sunk) | dynamic-update-slice | bytes 1572868 | tf_op jit(solution)/shard_map/while/body/jit(dynamic_update_index_in_dim)/dynamic_update_slice | solution.py:238
  848.7 6.5 fusion.76
  855.3 6.4 fusion.77
  861.7 12.7 add_convert_fusion
  874.5 11.2 convolution_convert_fusion
  885.8 12.3 convolution_convert_fusion.2
  898.1 10.2 convolution_convert_fusion.3
  908.3 8.4 convolution_convert_fusion.1
  935.9 40.0 %all-reduce = (f32[1536]{0:T(1024)}, f32[1536]{0:T(1024)}) all-reduce(f32[1536]{0:T(1024)S(1)} %get-tuple-element.234, f32[1536]{0:T(1024)S(1)} %copy-done.44), channel_id=1, replica_groups=mesh['dp'=8,'tensor'=4] {'dp','tensor'}, use_global_device_ids=true, to_apply=%region_16.17 | all-reduce | flops 3072 | bytes 24576 | tf_op jit(solution)/shard_map/psum | solution.py:270
  975.9 19.4 %reduce-scatter.7.cloned.1.call-done = bf16[512,1536]{1,0:T(8,128)(2,1)} async-done(((bf16[2048,1536]{1,0:T(8,128)(2,1)}), bf16[512,1536]{1,0:T(8,128)(2,1)}) %reduce-scatter.7.cloned.1.call-update) | async-done | bytes 1572880 | tf_op jit(solution)/shard_map/reduce_scatter | solution.py:171
  995.3 6.1 fusion.64
  1001.4 414.3 %all-reduce.4.cloned.1.call-done = (bf16[1536,384]{1,0:T(8,128)(2,1)}, bf16[1536,192]{0,1:T(8,128)(2,1)}, bf16[1536,192]{0,1:T(8,128)(2,1)}, bf16[384,1536]{1,0:...) async-done(((bf16[1536,384]{1,0:T(8,128)(2,1)}, bf16[1536,192]{0,1:T(8,128)(2,1)}, bf16[1536,192]{0,1:T(8,128)(2,1)}, ...) | async-done | bytes 12976144 | tf_op jit(solution)/shard_map/psum | solution.py:272
  (297 shorter events, 216.8 us)
Async XLA Ops:
  7.2 375.0 %copy-start = (bf16[1536,1024]{1,0:T(8,128)(2,1)S(1)}, bf16[1536,1024]{1,0:T(8,128)(2,1)}, u32[]{:S(2)}) copy-start(bf16[1536,1024]{1,0:T(8,128)(2,1)} %param.26) | copy-start | bytes 9437188
  7.2 54.2 %all-gather.4.cloned.1.call-start = ((), (), s32[]{:S(2)}) async-start(), calls=%async_computation.4 | async-start | bytes 7864320 | tf_op jit(solution)/shard_map/all_gather | solution.py:104
  12.2 256.3 %reduce-scatter.5.cloned.1.call-start = ((), (), s32[]{:S(2)}) async-start(), calls=%async_computation.5 | async-start | bytes 15728640 | tf_op jit(solution)/shard_map/reduce_scatter | solution.py:138
  15.2 55.7 %copy-start.12 = (f32[2048,48]{0,1:T(8,128)}, f32[2048,48]{0,1:T(8,128)S(1)}, u32[]{:S(2)}) copy-start(f32[2048,48]{0,1:T(8,128)S(1)} %get-tuple-element.312) | copy-start | bytes 1179652
  169.3 180.8 %all-gather.6.cloned.1.call-start = ((), (), s32[]{:S(2)}) async-start(), calls=%async_computation.7 | async-start | bytes 7864320 | tf_op jit(solution)/shard_map/all_gather | solution.py:178
  170.0 348.2 %reduce-scatter.9.cloned.1.call-start = ((), (), s32[]{:S(2)}) async-start(), calls=%async_computation.8 | async-start | bytes 15728640 | tf_op jit(solution)/shard_map/reduce_scatter | solution.py:187
  271.3 250.3 %copy-start.42 = (f32[512]{0:T(512)}, f32[512]{0:T(512)S(1)}, u32[]{:S(2)}) copy-start(f32[512]{0:T(512)S(1)} %add_rsqrt_fusion) | copy-start | bytes 6148
  277.3 69.3 %collective-permute-start = (bf16[512,1536]{1,0:T(8,128)(2,1)}, bf16[512,1536]{1,0:T(8,128)(2,1)}, u32[]{:S(2)}, u32[]{:S(2)}) collective-permute-start(bf16[512,1536]{1,0:T(8,128)(2,1)} %get-tuple-element.288), channel_id=1, source_target_pairs={{0,1},{1,2},{2,3},{3,0},{4,5},{5,6},{6,7},{7,4},{8,9},{9,10},{10,1... | collective-permute-start | bytes 4718600 | tf_op jit(solution)/shard_map/ppermute | solution.py:155
  277.3 88.1 %collective-permute-start.1 = (bf16[512,1536]{1,0:T(8,128)(2,1)}, bf16[512,1536]{1,0:T(8,128)(2,1)}, u32[]{:S(2)}, u32[]{:S(2)}) collective-permute-start(bf16[512,1536]{1,0:T(8,128)(2,1)} %get-tuple-element.288), channel_id=1, source_target_pairs={{0,3},{1,0},{2,1},{3,2},{4,7},{5,4},{6,5},{7,6},{8,11},{9,8},{10,9... | collective-permute-start | bytes 4718600 | tf_op jit(solution)/shard_map/ppermute | solution.py:158
  346.6 21.6 %collective-permute-start.2 = (bf16[512,1536]{1,0:T(8,128)(2,1)}, bf16[512,1536]{1,0:T(8,128)(2,1)}, u32[]{:S(2)}, u32[]{:S(2)}) collective-permute-start(bf16[512,1536]{1,0:T(8,128)(2,1)} %collective-permute-done), channel_id=1, source_target_pairs={{0,1},{1,2},{2,3},{3,0},{4,5},{5,6},{6,7},{7,4},{8,9},{9,10},{10,1... | collective-permute-start | bytes 4718600 | tf_op jit(solution)/shard_map/ppermute | solution.py:155
  370.8 11.3 copy-start.17
  398.5 8.7 copy-start.52
  419.5 98.8 %copy-start.7 = (f32[512,1536]{1,0:T(8,128)S(1)}, f32[512,1536]{1,0:T(8,128)}, u32[]{:S(2)}) copy-start(f32[512,1536]{1,0:T(8,128)} %copy-done.6) | copy-start | bytes 9437188
  419.5 150.8 %all-gather.8.cloned.1.call-start = ((), (), s32[]{:S(2)}) async-start(), calls=%async_computation.9 | async-start | bytes 7864320 | tf_op jit(solution)/shard_map/all_gather | solution.py:197
  523.8 409.1 %reduce-scatter.11.cloned.1.call-start = ((), (), s32[]{:S(2)}) async-start(), calls=%async_computation.10 | async-start | bytes 7864320 | tf_op jit(solution)/shard_map/reduce_scatter | solution.py:258
  625.4 6.4 copy-start.2
  625.4 6.4 copy-start.3
  634.5 16.9 %copy-start.4 = (f32[2048,2,96]{0,2,1:T(8,128)}, f32[2048,2,96]{0,2,1:T(8,128)S(1)}, u32[]{:S(2)}) copy-start(f32[2048,2,96]{0,2,1:T(8,128)S(1)} %fusion.157) | copy-start | bytes 4718596 | tf_op jit(solution)/shard_map/while
  634.5 16.9 %copy-start.31 = (s32[2048]{0:T(1024)S(1)}, s32[2048]{0:T(1024)}, u32[]{:S(2)}) copy-start(s32[2048]{0:T(1024)} %copy-done.30) | copy-start | bytes 24580 | tf_op jit(solution)/shard_map/while
  634.5 16.9 %copy-start.40 = (s32[4,512]{1,0:T(4,128)S(1)}, s32[4,512]{1,0:T(4,128)}, u32[]{:S(2)}) copy-start(s32[4,512]{1,0:T(4,128)} %copy-done.39) | copy-start | bytes 24580 | tf_op jit(solution)/shard_map/while
  688.5 6.4 copy-start.2
  688.5 6.4 copy-start.3
  697.6 16.9 %copy-start.4 = (f32[2048,2,96]{0,2,1:T(8,128)}, f32[2048,2,96]{0,2,1:T(8,128)S(1)}, u32[]{:S(2)}) copy-start(f32[2048,2,96]{0,2,1:T(8,128)S(1)} %fusion.157) | copy-start | bytes 4718596 | tf_op jit(solution)/shard_map/while
  697.6 16.9 %copy-start.31 = (s32[2048]{0:T(1024)S(1)}, s32[2048]{0:T(1024)}, u32[]{:S(2)}) copy-start(s32[2048]{0:T(1024)} %copy-done.30) | copy-start | bytes 24580 | tf_op jit(solution)/shard_map/while
  697.6 16.9 %copy-start.40 = (s32[4,512]{1,0:T(4,128)S(1)}, s32[4,512]{1,0:T(4,128)}, u32[]{:S(2)}) copy-start(s32[4,512]{1,0:T(4,128)} %copy-done.39) | copy-start | bytes 24580 | tf_op jit(solution)/shard_map/while
  751.6 6.4 copy-start.3
  760.7 16.9 %copy-start.4 = (f32[2048,2,96]{0,2,1:T(8,128)}, f32[2048,2,96]{0,2,1:T(8,128)S(1)}, u32[]{:S(2)}) copy-start(f32[2048,2,96]{0,2,1:T(8,128)S(1)} %fusion.157) | copy-start | bytes 4718596 | tf_op jit(solution)/shard_map/while
  760.7 16.9 %copy-start.31 = (s32[2048]{0:T(1024)S(1)}, s32[2048]{0:T(1024)}, u32[]{:S(2)}) copy-start(s32[2048]{0:T(1024)} %copy-done.30) | copy-start | bytes 24580 | tf_op jit(solution)/shard_map/while
  760.7 16.9 %copy-start.40 = (s32[4,512]{1,0:T(4,128)S(1)}, s32[4,512]{1,0:T(4,128)}, u32[]{:S(2)}) copy-start(s32[4,512]{1,0:T(4,128)} %copy-done.39) | copy-start | bytes 24580 | tf_op jit(solution)/shard_map/while
  814.7 6.4 copy-start.3
  823.8 16.9 %copy-start.4 = (f32[2048,2,96]{0,2,1:T(8,128)}, f32[2048,2,96]{0,2,1:T(8,128)S(1)}, u32[]{:S(2)}) copy-start(f32[2048,2,96]{0,2,1:T(8,128)S(1)} %fusion.157) | copy-start | bytes 4718596 | tf_op jit(solution)/shard_map/while
  823.8 16.9 %copy-start.31 = (s32[2048]{0:T(1024)S(1)}, s32[2048]{0:T(1024)}, u32[]{:S(2)}) copy-start(s32[2048]{0:T(1024)} %copy-done.30) | copy-start | bytes 24580 | tf_op jit(solution)/shard_map/while
  823.8 16.9 %copy-start.40 = (s32[4,512]{1,0:T(4,128)S(1)}, s32[4,512]{1,0:T(4,128)}, u32[]{:S(2)}) copy-start(s32[4,512]{1,0:T(4,128)} %copy-done.39) | copy-start | bytes 24580 | tf_op jit(solution)/shard_map/while
  848.6 6.6 copy-start.34
  855.3 6.4 copy-start.36
  874.4 120.9 %reduce-scatter.7.cloned.1.call-start = ((), (), s32[]{:S(2)}) async-start(), calls=%async_computation.6 | async-start | bytes 7864320 | tf_op jit(solution)/shard_map/reduce_scatter | solution.py:171
  885.8 530.0 %all-reduce.4.cloned.1.call-start = ((), (), s32[]{:S(2)}) async-start(), calls=%async_computation.11 | async-start | bytes 25952256 | tf_op jit(solution)/shard_map/psum | solution.py:272
  885.8 12.3 copy-start.53
  885.8 22.5 %slice-start.2 = ((s8[6291456]{0:T(1024)(128)(4,1)}), s8[4194304]{0:T(1024)(128)(4,1)S(1)}, s32[]{:S(2)}) async-start(s8[6291456]{0:T(1024)(128)(4,1)} %bitcast.262), calls=%async_computation.14 | async-start | bytes 8388608
  898.1 10.2 slice-start.3
  898.1 10.2 copy-start.54
  898.1 18.6 %slice-start = ((s8[6291456]{0:T(1024)(128)(4,1)}), s8[4194304]{0:T(1024)(128)(4,1)S(1)}, s32[]{:S(2)}) async-start(s8[6291456]{0:T(1024)(128)(4,1)} %bitcast.260), calls=%async_computation.12 | async-start | bytes 8388608
  908.3 8.5 slice-start.1
  929.4 6.5 copy-start.44
  929.4 65.9 %copy-start.8 = (f32[512,1536]{1,0:T(8,128)S(1)}, f32[512,1536]{1,0:T(8,128)}, u32[]{:S(2)}) copy-start(f32[512,1536]{1,0:T(8,128)} %copy-done.6) | copy-start | bytes 9437188
  929.4 65.9 %copy-start.38 = (f32[1536]{0:T(1024)S(1)}, f32[1536]{0:T(1024)}, u32[]{:S(2)}) copy-start(f32[1536]{0:T(1024)} %param.25) | copy-start | bytes 18436
  929.4 65.9 %copy-start.43 = (f32[512]{0:T(512)S(1)}, f32[512]{0:T(512)}, u32[]{:S(2)}) copy-start(f32[512]{0:T(512)} %copy-done.42) | copy-start | bytes 6148
  929.4 65.9 %copy-start.48 = (f32[512]{0:T(512)S(1)}, f32[512]{0:T(512)}, u32[]{:S(2)}) copy-start(f32[512]{0:T(512)} %copy-done.47) | copy-start | bytes 6148
  (48 other events, 150.8 us)
Sparse Core Ops, SparseCore 0:
  12.3 49.0 all-gather.3
  169.4 99.0 reduce-scatter.4
  270.1 80.0 all-gather.5
  419.6 98.5 reduce-scatter.8
  523.9 46.3 all-gather.7
  874.5 58.3 reduce-scatter.10
  936.2 59.0 reduce-scatter.6
  1002.1 413.5 all-reduce.3
